TPU v7x, 512 devices: a whole 4x4x16 slice. The times are simulated.
512 devices in a mesh: dp: 32 (over z_lo, y), mp: 16 (over x, z_hi, core).
Axes of the slice: x: 4, y: 4, z: 16 (z_hi: 2, z_lo: 8; z = z_hi * 8 + z_lo), core: 2. Of those that a mesh axis runs over, the one named last changes fastest.
Arguments:
- tokens: bfloat16 [32768, 8192], P('dp', 'mp'), may hold values from -6 to 6
- cotangent: bfloat16 [32768, 8192], P('dp', 'mp'), may hold values from -6 to 6
- first_factor: bfloat16 [64, 128, 128], P('mp'), may hold values from -0.5 to 0.5
- second_factor: bfloat16 [64, 128, 128], P('mp'), may hold values from -0.5 to 0.5
Outputs:
- output: bfloat16 [32768, 8192], P('dp', 'mp')
- input_grad: bfloat16 [32768, 8192], P('dp', 'mp')
- first_grad: float32 [64, 128, 128], P('mp')
- second_grad: float32 [64, 128, 128], P('mp')
All inputs are finite; a program needn't handle non-finite values.
Results may differ from a plain program's by a relative error of at most 0.007.
Values may be sent and summed in bfloat16 or wider, within the bound.
A program may use at most 64 MiB of HBM per device.

v0:
```python
import jax
import jax.numpy as jnp
from jax import lax
from jax.sharding import PartitionSpec as P


def gate_terms(xs, grads, zed):
    xf = xs.astype(jnp.float32)
    gf = grads.astype(jnp.float32)
    zf = zed.astype(jnp.float32)
    sig = jax.nn.sigmoid(xf)
    silu = xf * sig
    output = (zf * silu).astype(jnp.bfloat16)
    grad_z = (gf * silu).astype(jnp.bfloat16)
    gate_grad = (gf * zf * sig * (1.0 + xf * (1.0 - sig))).astype(jnp.bfloat16)
    return (output, grad_z, gate_grad)


def shards(tokens, cotangent, first_factor, second_factor):
    nloc, blk, _ = first_factor.shape
    groups = lax.axis_size("mp")
    nblk = nloc * groups
    ratio = blk // nblk
    rows = tokens.shape[0]
    x_three = tokens.reshape(rows, nloc, blk).transpose(1, 2, 0)
    g_three = cotangent.reshape(rows, nloc, blk).transpose(1, 2, 0)
    x_four = x_three.reshape(nloc, nblk, ratio, rows)
    g_four = g_three.reshape(nloc, nblk, ratio, rows)
    w_first = first_factor.reshape(nloc, blk, nblk, ratio)
    w_second = second_factor.reshape(nloc, ratio, nblk, nblk, ratio)
    hidden = jnp.einsum(
        "ixn,ixjc->ijcn", x_three, w_first, preferred_element_type=jnp.float32
    ).astype(jnp.bfloat16)
    gathered = lax.all_to_all(hidden, "mp", split_axis=1, concat_axis=0, tiled=True)
    result = jnp.einsum(
        "ijcn,jciab->ajbn", gathered, w_second, preferred_element_type=jnp.float32
    ).astype(jnp.bfloat16)
    zed = lax.all_to_all(result, "mp", split_axis=0, concat_axis=1, tiled=True)
    output, grad_z, gate_grad = gate_terms(x_four, g_four, zed)
    grad_mixed = lax.all_to_all(grad_z, "mp", split_axis=1, concat_axis=0, tiled=True)
    second_term = jnp.einsum(
        "ijcn,ajbn->jciab", gathered, grad_mixed, preferred_element_type=jnp.float32
    )
    grad_u = jnp.einsum(
        "ajbn,jciab->ijcn", grad_mixed, w_second, preferred_element_type=jnp.float32
    ).astype(jnp.bfloat16)
    grad_hidden = lax.all_to_all(grad_u, "mp", split_axis=0, concat_axis=1, tiled=True)
    first_term = jnp.einsum(
        "ixn,ijcn->ixjc", x_three, grad_hidden, preferred_element_type=jnp.float32
    )
    input_grad = jnp.einsum(
        "ijcn,ixjc->ixn", grad_hidden, w_first, preferred_element_type=jnp.float32
    )
    input_grad = (input_grad + gate_grad.reshape(nloc, blk, rows).astype(jnp.float32)).astype(
        jnp.bfloat16
    )
    scale = 1.0 / jnp.sqrt(jnp.float32(rows * lax.axis_size("dp")))
    first_local = first_term.reshape(nloc, blk, blk) * scale
    second_local = second_term.reshape(nloc, blk, blk) * scale
    first_grad, second_grad = lax.psum((first_local, second_local), "dp")
    output = output.reshape(nloc * blk, rows).transpose(1, 0)
    input_grad = input_grad.reshape(nloc * blk, rows).transpose(1, 0)
    return (output, input_grad, first_grad, second_grad)


def solution(mesh):
    return jax.shard_map(
        shards,
        mesh=mesh,
        in_specs=(P("dp", "mp"), P("dp", "mp"), P("mp", None, None), P("mp", None, None)),
        out_specs=(P("dp", "mp"), P("dp", "mp"), P("mp", None, None), P("mp", None, None)),
        check_vma=False,
    )
```

profile of v0, /device:TPU:2, one launch (start us, length us, event | category | flops | bytes accessed | tf_op | source)
XLA Modules:
  0.0 714.3 jit_solution(8183532458692884184)
XLA Ops:
  7.2 1.5 copy.88
  8.7 2.1 copy.98
  10.8 1.5 copy.96
  12.3 1.4 copy.97
  14.7 2.5 fusion.5
  17.2 2.1 copy.102
  19.2 18.1 %all-to-all-start.2 = ((bf16[4,64,2,1024]{3,2,0,1:T(2,128)(2,1)}), bf16[4,64,2,1024]{3,2,0,1:T(2,128)(2,1)S(1)}, u32[]{:S(2)}, u32[]{:S(2)}) async-start(bf16[4,64,2,1024]{3,2,0,1:T(2,128)(2,1)} %copy.102), calls=%async_computation.2 | async-start | bytes 2097152 | tf_op jit(solution)/shard_map/all_to_all | solution.py:40
  37.9 2.1 copy.90
  40.0 24.7 %all-to-all-done.2 = bf16[4,64,2,1024]{3,2,0,1:T(2,128)(2,1)S(1)} async-done(((bf16[4,64,2,1024]{3,2,0,1:T(2,128)(2,1)}), bf16[4,64,2,1024]{3,2,0,1:T(2,128)(2,1)S(1)}, u32[]{:S(2)}, u32[]{:S(2)}) %all-to-all-start.2) | async-done | bytes 1048608 | tf_op jit(solution)/shard_map/all_to_all | solution.py:40
  64.7 6.7 all-to-all-start
  73.2 1.4 copy.104
  74.6 1.3 reshape.68
  76.4 2.1 copy.106
  78.5 22.8 %all-to-all-done = bf16[4,64,2,1024]{3,2,0,1:T(2,128)(2,1)S(1)} async-done(((bf16[4,64,2,1024]{3,2,0,1:T(2,128)(2,1)}), bf16[4,64,2,1024]{3,2,0,1:T(2,128)(2,1)S(1)}, u32[]{:S(2)}, u32[]{:S(2)}) %all-to-all-start) | async-done | bytes 1048608 | tf_op jit(solution)/shard_map/all_to_all | solution.py:34
  101.3 14.6 %all-to-all-start.3 = ((bf16[64,4,2,1024]{3,2,1,0:T(2,128)(2,1)}), bf16[64,4,2,1024]{3,2,1,0:T(2,128)(2,1)}, u32[]{:S(2)}, u32[]{:S(2)}) async-start(bf16[64,4,2,1024]{3,2,1,0:T(2,128)(2,1)} %copy.106), calls=%async_computation.3 | async-start | bytes 2097152 | tf_op jit(solution)/shard_map/all_to_all | solution.py:47
  115.8 1.4 copy.139
  117.2 1.3 reshape.66
  119.0 2.1 copy.94
  121.1 35.9 %all-to-all-done.3 = bf16[64,4,2,1024]{3,2,1,0:T(2,128)(2,1)} async-done(((bf16[64,4,2,1024]{3,2,1,0:T(2,128)(2,1)}), bf16[64,4,2,1024]{3,2,1,0:T(2,128)(2,1)}, u32[]{:S(2)}, u32[]{:S(2)}) %all-to-all-start.3) | async-done | bytes 1048608 | tf_op jit(solution)/shard_map/all_to_all | solution.py:47
  157.0 5.7 all-to-all-start.1
  164.9 1.7 copy.138
  168.2 33.7 %all-to-all-done.1 = bf16[64,4,2,1024]{3,2,1,0:T(2,128)(2,1)} async-done(((bf16[64,4,2,1024]{3,2,1,0:T(2,128)(2,1)}), bf16[64,4,2,1024]{3,2,1,0:T(2,128)(2,1)}, u32[]{:S(2)}, u32[]{:S(2)}) %all-to-all-start.1) | async-done | bytes 1048608 | tf_op jit(solution)/shard_map/all_to_all | solution.py:38
  201.9 2.1 copy_bitcast_fusion
  204.0 2.5 reshape.60
  206.5 4.7 fusion
  211.1 2.4 reshape.56
  213.6 2.4 copy.109
  216.0 1.7 fusion.6
  217.7 2.3 copy.112
  219.9 483.9 %all-reduce.3.cloned.1.call-done = (f32[4,128,128]{1,2,0:T(8,128)}, f32[4,128,128]{1,2,0:T(8,128)}) async-done(((f32[4,128,128]{1,2,0:T(8,128)}, f32[4,128,128]{1,2,0:T(8,128)}), (f32[4,128,128]{1,2,0:T(8,128)}, f32[4,128,128]{1,2,0:T(8,128)})) %all-reduce.3.cloned.1.call-update) | async-done | bytes 524304 | tf_op jit(solution)/shard_map/psum | solution.py:60
  703.9 1.8 copy.113
  705.6 1.8 copy.114
  (26 shorter events, 8.1 us)
Async XLA Ops:
  12.3 1.4 copy-start
  12.3 2.3 copy-start.2
  17.2 20.2 %copy-start.4 = (bf16[4,128,128]{2,1,0:T(8,128)(2,1)S(1)}, bf16[4,128,128]{2,1,0:T(8,128)(2,1)}, u32[]{:S(2)}) copy-start(bf16[4,128,128]{2,1,0:T(8,128)(2,1)} %param.6) | copy-start | bytes 393220
  19.2 45.5 %all-to-all-start.2 = ((bf16[4,64,2,1024]{3,2,0,1:T(2,128)(2,1)}), bf16[4,64,2,1024]{3,2,0,1:T(2,128)(2,1)S(1)}, u32[]{:S(2)}, u32[]{:S(2)}) async-start(bf16[4,64,2,1024]{3,2,0,1:T(2,128)(2,1)} %copy.102), calls=%async_computation.2 | async-start | bytes 2097152 | tf_op jit(solution)/shard_map/all_to_all | solution.py:40
  37.9 33.5 %copy-start.5 = (bf16[4,128,128]{2,1,0:T(8,128)(2,1)S(1)}, bf16[4,128,128]{2,1,0:T(8,128)(2,1)}, u32[]{:S(2)}) copy-start(bf16[4,128,128]{2,1,0:T(8,128)(2,1)} %param.7) | copy-start | bytes 393220
  64.7 36.5 %all-to-all-start = ((bf16[4,64,2,1024]{3,2,0,1:T(2,128)(2,1)}), bf16[4,64,2,1024]{3,2,0,1:T(2,128)(2,1)S(1)}, u32[]{:S(2)}, u32[]{:S(2)}) async-start(bf16[4,64,2,1024]{3,2,0,1:T(2,128)(2,1)} %copy.90), calls=%async_computation | async-start | bytes 2097152 | tf_op jit(solution)/shard_map/all_to_all | solution.py:34
  101.3 55.7 %all-to-all-start.3 = ((bf16[64,4,2,1024]{3,2,1,0:T(2,128)(2,1)}), bf16[64,4,2,1024]{3,2,1,0:T(2,128)(2,1)}, u32[]{:S(2)}, u32[]{:S(2)}) async-start(bf16[64,4,2,1024]{3,2,1,0:T(2,128)(2,1)} %copy.106), calls=%async_computation.3 | async-start | bytes 2097152 | tf_op jit(solution)/shard_map/all_to_all | solution.py:47
  157.0 44.9 %all-to-all-start.1 = ((bf16[64,4,2,1024]{3,2,1,0:T(2,128)(2,1)}), bf16[64,4,2,1024]{3,2,1,0:T(2,128)(2,1)}, u32[]{:S(2)}, u32[]{:S(2)}) async-start(bf16[64,4,2,1024]{3,2,1,0:T(2,128)(2,1)} %copy.94), calls=%async_computation.1 | async-start | bytes 2097152 | tf_op jit(solution)/shard_map/all_to_all | solution.py:38
  162.7 541.1 %all-reduce.3.cloned.1.call-start = ((), (), s32[]{:S(2)}) async-start(), calls=%async_computation.4 | async-start | bytes 1048576 | tf_op jit(solution)/shard_map/psum | solution.py:60
  166.9 35.0 %copy-start.3 = (bf16[4,64,2,1024]{3,1,2,0:T(8,128)(2,1)}, bf16[4,64,2,1024]{3,1,2,0:T(8,128)(2,1)S(1)}, u32[]{:S(2)}) copy-start(bf16[4,64,2,1024]{3,1,2,0:T(8,128)(2,1)S(1)} %all_to_all.58) | copy-start | bytes 3145732
  213.6 2.4 copy-start.1
Sparse Core Ops, SparseCore 0:
  206.6 497.2 all-reduce.2
where the time goes:
time: 715 us; the launch traced here: 714 us
  waiting for transfers between devices  601 us (84%)
  starting transfers between devices  45.1 us (6%)
  local copies, waits for them, and re-layouts  40.5 us (6%)
  between operations  14.2 us (2%)
  matrix products  7.16 us (1%)
    psum x1, waiting for transfers between devices, shards(): first_grad, second_grad = lax.psum((first_local, second_local), 'dp')  484 us
    all_to_all x1, waiting for transfers between devices, shards(): lax.all_to_all(grad_u, 'mp', split_axis=0, concat_axis=1, tiled=True)  35.9 us
    all_to_all x1, waiting for transfers between devices, shards(): zed = lax.all_to_all(result, 'mp', split_axis=0, concat_axis=1, tiled=True)  33.7 us
    all_to_all x1, waiting for transfers between devices, shards(): lax.all_to_all(grad_z, 'mp', split_axis=1, concat_axis=0, tiled=True)  24.7 us
    all_to_all x1, waiting for transfers between devices, shards(): lax.all_to_all(hidden, 'mp', split_axis=1, concat_axis=0, tiled=True)  22.8 us
    all_to_all x1, starting transfers between devices, shards(): lax.all_to_all(grad_z, 'mp', split_axis=1, concat_axis=0, tiled=True)  18.1 us
    all_to_all x1, starting transfers between devices, shards(): lax.all_to_all(grad_u, 'mp', split_axis=0, concat_axis=1, tiled=True)  14.6 us
  transfers between devices with their start and end apart: 5, of which 5 were waited for; matrix products, arithmetic and copies ran while one was open for 5% of the time, Pallas kernels for 0%

commit v1 on v0

v1 whole, which is shorter than its diff:
```python
import jax
import jax.numpy as jnp
from jax import lax
from jax.experimental import pallas as pl
from jax.experimental.pallas import tpu as pltpu
from jax.sharding import PartitionSpec as P

MESH = pl.DeviceIdType.MESH
BF = jnp.bfloat16
F32 = jnp.float32
NT = (((1,), (1,)), ((), ()))
NN = (((1,), (0,)), ((), ()))


def dot(left, right, form=NN):
    return lax.dot_general(left, right, form, preferred_element_type=F32)


def iota(shape, axis):
    return lax.broadcasted_iota(jnp.int32, shape, axis)


def swap_matrix():
    row, col = iota((128, 128), 0), iota((128, 128), 1)
    source = (row & 0b1100111) + ((row & 8) << 1) + ((row & 16) >> 1)
    return (col == source).astype(BF)


def block_of(position, plane):
    above = position >> 5
    absolute = (above + plane) & 1
    return ((position >> 3) & 3) * 16 + absolute * 8 + (position & 7)


def column_ab(code, plane):
    return block_of(code >> 4, plane) * 2 + (code & 1)


def column_ci(code, plane):
    return (code & 1) * 64 + block_of(code >> 4, plane)


def kernel(
    chunks,
    tok, cot, w1, w2,
    out, grad_in, first_out, second_out,
    stage, held, back, landed, xt, gt, w1t, w1p, wpair, wf, wb, sel_ab, sel_ci, acc_first, acc_second, mid,
    send_a, recv_a, send_z, recv_z, send_b, recv_b, own_sem, w_sem,
):
    n = tok.shape[0] // chunks
    d, m = lax.axis_index("dp"), lax.axis_index("mp")
    x, plane, core = m // 4, (m // 2) % 2, m % 2
    me = x * 2 + core
    mate = (d, m + 2 - 4 * plane)

    def peer(k):
        q = (me + k) % 8
        return q, (d, (q // 2) * 4 + plane * 2 + q % 2)

    barrier = pltpu.get_barrier_semaphore()
    for k in range(1, 8):
        pl.semaphore_signal(barrier, inc=1, device_id=peer(k)[1], device_id_type=MESH)
    pl.semaphore_signal(barrier, inc=1, device_id=mate, device_id_type=MESH)

    def give_weights():
        return pltpu.make_async_remote_copy(
            w2, wpair.at[plane], w_sem.at[0], w_sem.at[1], device_id=mate, device_id_type=MESH
        )

    def keep_weights():
        return pltpu.make_async_copy(w2, wpair.at[plane], w_sem.at[2])

    def out_copy(c, k):
        q, device = peer(k)
        return pltpu.make_async_remote_copy(
            stage.at[c, q], held.at[c, 0, :, pl.ds(4 * me, 4)],
            send_a.at[c, k], recv_a.at[c, k], device_id=device, device_id_type=MESH,
        )

    def out_own(c):
        return pltpu.make_async_copy(stage.at[c, me], held.at[c, 0, :, pl.ds(4 * me, 4)], own_sem.at[c, 0])

    def plane_copy(c, kind):
        return pltpu.make_async_remote_copy(
            held.at[c, 0, kind], held.at[c, 1, kind],
            send_z.at[c, kind], recv_z.at[c, kind], device_id=mate, device_id_type=MESH,
        )

    def back_copy(c, k):
        q, device = peer(k)
        return pltpu.make_async_remote_copy(
            back.at[c, q], landed.at[c, :, :, me],
            send_b.at[c, k], recv_b.at[c, k], device_id=device, device_id_type=MESH,
        )

    def back_own(c):
        return pltpu.make_async_copy(back.at[c, me], landed.at[c, :, :, me], own_sem.at[c, 1])

    swap = swap_matrix()
    for i in range(4):
        half = dot(swap, w1[i], NT).astype(BF)
        w1t[i] = dot(half, swap).astype(BF)
        half = dot(swap, w1[i]).astype(BF)
        w1p[i] = dot(half, swap).astype(BF)
    acc_first[...] = jnp.zeros_like(acc_first)
    pl.semaphore_wait(barrier, 8)
    give_weights().start()
    keep_weights().start()

    def to_mate(c):
        for k in range(1, 8):
            out_copy(c, k).wait_recv()
        out_own(c).wait()
        for kind in range(2):
            plane_copy(c, kind).start()

    def begin(c, _):
        rows = pl.ds(pl.multiple_of(c * n, n), n)
        for i in range(4):
            cols = pl.ds(128 * i, 128)
            xf = dot(swap, tok[rows, cols], NT)
            gf = dot(swap, cot[rows, cols], NT)
            xb = xf.astype(BF)
            xt[c, i] = xb
            gt[c, i] = gf.astype(BF)
            hidden = dot(w1t[i], xb).astype(BF)
            grad_z = (gf * (xf * jax.nn.sigmoid(xf))).astype(BF)
            stage[c, :, 0, i] = hidden.reshape(8, 16, n)
            stage[c, :, 1, i] = grad_z.reshape(8, 16, n)
        out_own(c).start()
        for k in range(1, 8):
            out_copy(c, k).start()

        @pl.when(c >= 1)
        def _():
            to_mate(c - 1)

        return 0

    lax.fori_loop(0, chunks, begin, 0)
    to_mate(chunks - 1)

    rows_q, cols_q = iota((128, 1024), 0), iota((128, 1024), 1)
    sel_ab[...] = (rows_q == column_ab(cols_q, plane)).astype(BF)
    sel_ci[...] = (rows_q == column_ci(cols_q, plane)).astype(BF)
    give_weights().wait_recv()
    keep_weights().wait()

    def spread(b, _):
        start = pl.multiple_of(b * 128, 128)
        code = iota((128, 128), 0) + b * 128
        lane = iota((128, 128), 1)
        pick_ab = (lane == column_ab(code, plane)).astype(BF)
        pick_ci = (lane == column_ci(code, plane)).astype(BF)
        group = (code >> 1) & 7
        forward = jnp.zeros((128, 128), F32)
        backward = jnp.zeros((128, 128), F32)
        for j in range(8):
            block = wpair[j // 4, j % 4]
            forward = jnp.where(group == j, dot(pick_ab, block, NT), forward)
            backward = jnp.where(group == j, dot(pick_ci, block), backward)
        same = ((iota((128, 1024), 0) >> 1) & 7) == ((cols_q >> 1) & 7)
        wf[pl.ds(start, 128)] = jnp.where(same, dot(forward.astype(BF), sel_ci[...]), 0.0).astype(BF)
        wb[pl.ds(start, 128)] = jnp.where(same, dot(backward.astype(BF), sel_ab[...]), 0.0).astype(BF)
        return 0

    lax.fori_loop(0, 4, spread, 0)
    acc_second[...] = jnp.zeros_like(acc_second)
    eye = (iota((n, n), 0) == iota((n, n), 1)).astype(BF)

    def finish(c):
        for k in range(1, 8):
            back_copy(c, k).wait_recv()
        back_own(c).wait()
        rows = pl.ds(pl.multiple_of(c * n, n), n)
        for i in range(4):
            cols = pl.ds(128 * i, 128)
            xb = xt[c, i]
            xf = xb.astype(F32)
            gf = gt[c, i].astype(F32)
            zf = landed[c, 0, i].reshape(128, n).astype(F32)
            gu = landed[c, 1, i].reshape(128, n)
            sig = jax.nn.sigmoid(xf)
            y = (zf * (xf * sig)).astype(BF)
            gate = (gf * zf * sig * (1.0 + xf * (1.0 - sig))).astype(BF)
            gx = (dot(w1p[i], gu) + gate.astype(F32)).astype(BF)
            acc_first[i] += dot(xb, gu, NT)
            out[rows, cols] = dot(dot(eye, y, NT).astype(BF), swap).astype(BF)
            grad_in[rows, cols] = dot(dot(eye, gx, NT).astype(BF), swap).astype(BF)

    def middle(c, _):
        for kind in range(2):
            plane_copy(c, kind).wait_recv()
        hidden = held[c, :, 0].reshape(1024, n)
        grad_mixed = held[c, :, 1].reshape(1024, n)
        back[c, :, 0] = dot(wf[...], hidden).astype(BF).reshape(8, 4, 16, n)
        back[c, :, 1] = dot(wb[...], grad_mixed).astype(BF).reshape(8, 4, 16, n)
        back_own(c).start()
        for k in range(1, 8):
            back_copy(c, k).start()
        acc_second[...] += dot(hidden, grad_mixed, NT)

        @pl.when(c >= 1)
        def _():
            finish(c - 1)

        return 0

    lax.fori_loop(0, chunks, middle, 0)

    def gather(b, _):
        start = pl.multiple_of(b * 128, 128)
        code = iota((128, 1024), 0)
        same = ((code >> 1) & 7) == ((cols_q >> 1) & 7)
        part = jnp.where(same, acc_second[pl.ds(start, 128)], 0.0).astype(BF)
        mid[pl.ds(start, 128)] = dot(part, sel_ab[...], NT).astype(BF)
        return 0

    lax.fori_loop(0, 8, gather, 0)
    for j in range(4):
        chosen = ((cols_q >> 1) & 7) == plane * 4 + j
        pick = jnp.where(chosen, sel_ci[...].astype(F32), 0.0).astype(BF)
        second_out[j] = dot(pick, mid[...]).astype(BF)
    finish(chunks - 1)
    for i in range(4):
        half = dot(swap, acc_first[i].astype(BF)).astype(BF)
        first_out[i] = dot(half, swap).astype(BF)

    def drain(c, _):
        for k in range(1, 8):
            out_copy(c, k).wait_send()
            back_copy(c, k).wait_send()
        for kind in range(2):
            plane_copy(c, kind).wait_send()
        return 0

    lax.fori_loop(0, chunks, drain, 0)
    give_weights().wait_send()


def shards(tokens, cotangent, first_factor, second_factor):
    rows, width = tokens.shape
    chunks = 8
    n = rows // chunks
    V = pl.BlockSpec(memory_space=pltpu.VMEM)
    dma = pltpu.SemaphoreType.DMA
    small = jax.ShapeDtypeStruct(first_factor.shape, BF)
    wide = jax.ShapeDtypeStruct((rows, width), BF)
    output, input_grad, first, second = pl.pallas_call(
        lambda *refs: kernel(chunks, *refs),
        out_shape=(wide, wide, small, small),
        in_specs=[V] * 4,
        out_specs=(V,) * 4,
        scratch_shapes=[
            pltpu.VMEM((chunks, 8, 2, 4, 16, n), BF),
            pltpu.VMEM((chunks, 2, 2, 32, 16, n), BF),
            pltpu.VMEM((chunks, 8, 2, 4, 16, n), BF),
            pltpu.VMEM((chunks, 2, 4, 8, 16, n), BF),
            pltpu.VMEM((chunks, 4, 128, n), BF),
            pltpu.VMEM((chunks, 4, 128, n), BF),
            pltpu.VMEM((4, 128, 128), BF),
            pltpu.VMEM((4, 128, 128), BF),
            pltpu.VMEM((2, 4, 128, 128), BF),
            pltpu.VMEM((512, 1024), BF),
            pltpu.VMEM((512, 1024), BF),
            pltpu.VMEM((128, 1024), BF),
            pltpu.VMEM((128, 1024), BF),
            pltpu.VMEM((4, 128, 128), F32),
            pltpu.VMEM((1024, 1024), F32),
            pltpu.VMEM((1024, 128), BF),
            dma((chunks, 8)),
            dma((chunks, 8)),
            dma((chunks, 2)),
            dma((chunks, 2)),
            dma((chunks, 8)),
            dma((chunks, 8)),
            dma((chunks, 2)),
            dma((3,)),
        ],
        compiler_params=pltpu.CompilerParams(collective_id=0, has_side_effects=True),
        name="mixing",
    )(tokens, cotangent, first_factor, second_factor)
    scale = 1.0 / jnp.sqrt(jnp.float32(rows * lax.axis_size("dp")))
    first_grad, second_grad = lax.psum((first.astype(F32) * scale, second.astype(F32) * scale), "dp")
    return (output, input_grad, first_grad, second_grad)


def solution(mesh):
    return jax.shard_map(
        shards,
        mesh=mesh,
        in_specs=(P("dp", "mp"), P("dp", "mp"), P("mp", None, None), P("mp", None, None)),
        out_specs=(P("dp", "mp"), P("dp", "mp"), P("mp", None, None), P("mp", None, None)),
        check_vma=False,
    )
```

time: 715 us -> 694 us (0.971)
  Pallas kernels: 0 us -> 210 us
  waiting for transfers between devices: 601 us -> 463 us
  starting transfers between devices: 45.1 us -> 0.04 us
  local copies, waits for them, and re-layouts: 40.5 us -> 4.44 us
  matrix products: 7.16 us -> 0 us
    pallas_call x0 -> x1, Pallas kernels: none -> 210 us  [shards(): pl.pallas_call(lambda *refs: kernel(chunks, *refs), out_shape=(wide, wide...]
    all_to_all x4 -> x0, waiting for transfers between devices: 117 us -> none  [the longest x1 35.9 us: shards(): lax.all_to_all(grad_u, 'mp', split_axis=0, concat_axis=1, tiled=True)]
    all_to_all x4 -> x0, starting transfers between devices: 45.1 us -> none  [the longest x1 18.1 us: shards(): lax.all_to_all(grad_z, 'mp', split_axis=1, concat_axis=0, tiled=True)]
    psum x1, waiting for transfers between devices: 484 us -> 463 us  [shards(): lax.psum((first.astype(F32) * scale, second.astype(F32) * scale), 'dp')]
    convert_element_type x9 -> x0, local copies, waits for them, and re-layouts: 18.1 us -> none  [the longest x2 4.92 us: gate_terms(): zf = zed.astype(jnp.float32)]
    all_to_all x6 -> x0, local copies, waits for them, and re-layouts: 7.39 us -> none  [the longest x2 2.71 us: shards(): lax.all_to_all(grad_z, 'mp', split_axis=1, concat_axis=0, tiled=True)]
    dot_general x6 -> x0, matrix products: 7.16 us -> none  [the longest x1 4.65 us: shards(): jnp.einsum('ijcn,ixjc->ixn', grad_hidden, w_first, preferred_element_type...]
  transfers between devices with their start and end apart: 5 -> 1, of which waited for: 5 -> 1; matrix products, arithmetic and copies ran while one was open for 5% -> 0% of each run, Pallas kernels for 0% -> 0%
where the time goes in v1:
time: 694 us; the launch traced here: 693 us
  waiting for transfers between devices  463 us (67%)
  Pallas kernels  210 us (30%)
  between operations  14 us (2%)
    psum x1, waiting for transfers between devices, shards(): lax.psum((first.astype(F32) * scale, second.astype(F32) * scale), 'dp')  463 us
    pallas_call x1, Pallas kernels, shards(): pl.pallas_call(lambda *refs: kernel(chunks, *refs), out_shape=(wide, wide...  210 us
  transfers between devices with their start and end apart: 1, of which 1 were waited for; matrix products, arithmetic and copies ran while one was open for 0% of the time, Pallas kernels for 0%

profile of v1, /device:TPU:2, one launch (start us, length us, event | category | flops | bytes accessed | tf_op | source)
XLA Modules:
  0.0 693.4 jit_solution(6807272454817938362)
XLA Ops:
  7.2 0.0 all-reduce.3.cloned.1.call-start
  7.2 210.4 %mixing.1 = (bf16[1024,512]{1,0:T(8,128)(2,1)}, bf16[1024,512]{1,0:T(8,128)(2,1)}, bf16[4,128,128]{2,1,0:T(8,128)(2,1)}, bf16[4,128,128]{2,1,0:T(8,128)(2,1)}) custom-call(bf16[1024,512]{1,0:T(8,128)(2,1)} %refs_0_.1, bf16[1024,512]{1,0:T(8,128)(2,1)} %refs_1_.1, bf16[4,128,128]{2,1,0:T(8,128)(2,1)} %refs_2_.1, bf16[4,128,128]{2,1,0:T(8,128)(2,1)} %refs_3_.1), custom_call_target="tpu_custom_call" | custom-call | tf_op jit(solution)/shard_map/mixing/pallas_call | solution.py:249
  217.6 0.0 copy-start.1
  217.6 1.9 convert_multiply_fusion
  219.5 0.0 all-reduce.3.cloned.1.call-update
  219.5 462.6 %all-reduce.3.cloned.1.call-done = (f32[4,128,128]{2,1,0:T(8,128)}, f32[4,128,128]{2,1,0:T(8,128)}) async-done(((f32[4,128,128]{2,1,0:T(8,128)}, f32[4,128,128]{2,1,0:T(8,128)}), (f32[4,128,128]{2,1,0:T(8,128)}, f32[4,128,128]{2,1,0:T(8,128)})) %all-reduce.3.cloned.1.call-update) | async-done | bytes 524304 | tf_op jit(solution)/shard_map/psum | solution.py:284
  682.1 0.0 copy-done.1
  682.1 0.0 copy-start
  682.1 1.0 copy.12
  683.1 0.6 copy-done
  683.7 0.0 copy-start.3
  683.7 1.0 copy.13
  684.7 0.1 copy-done.3
  684.8 0.0 copy-start.2
  684.8 0.7 copy.14
  685.5 0.3 copy-done.2
  685.9 0.7 copy.15
Async XLA Ops:
  7.2 675.0 %all-reduce.3.cloned.1.call-start = ((), (), s32[]{:S(2)}) async-start(), calls=%async_computation | async-start | bytes 1048576 | tf_op jit(solution)/shard_map/psum | solution.py:284
  217.6 464.5 %copy-start.1 = (bf16[1024,512]{1,0:T(8,128)(2,1)S(1)}, bf16[1024,512]{1,0:T(8,128)(2,1)}, u32[]{:S(2)}) copy-start(bf16[1024,512]{1,0:T(8,128)(2,1)} %get-tuple-element.20) | copy-start | bytes 3145732
  682.1 1.6 copy-start
  683.7 1.1 copy-start.3
  684.8 1.0 copy-start.2
Sparse Core Ops, SparseCore 0:
  219.7 462.4 all-reduce.2

commit v2 on v1

--- a/solution.py
+++ b/solution.py
@@ -45,13 +45,24 @@
     tok, cot, w1, w2,
     out, grad_in, first_out, second_out,
     stage, held, back, landed, xt, gt, w1t, w1p, wpair, wf, wb, sel_ab, sel_ci, acc_first, acc_second, mid,
-    send_a, recv_a, send_z, recv_z, send_b, recv_b, own_sem, w_sem,
+    part, from_y, piece, from_z, whole, every,
+    send_a, recv_a, send_z, recv_z, send_b, recv_b, own_sem, w_send, w_recv, y_send, y_recv, z_send, z_recv, end_send, end_recv,
 ):
     n = tok.shape[0] // chunks
     d, m = lax.axis_index("dp"), lax.axis_index("mp")
     x, plane, core = m // 4, (m // 2) % 2, m % 2
     me = x * 2 + core
     mate = (d, m + 2 - 4 * plane)
+    zl, y = d // 4, d % 4
+    scale = 1.0 / jnp.sqrt(jnp.float32(tok.shape[0] * 32))
+
+    def along_y(k):
+        q = (y + k) % 4
+        return q, (zl * 4 + q, m)
+
+    def along_z(k):
+        q = (zl + k) % 8
+        return q, (q * 4 + y, m)
 
     def peer(k):
         q = (me + k) % 8
@@ -61,14 +72,50 @@
     for k in range(1, 8):
         pl.semaphore_signal(barrier, inc=1, device_id=peer(k)[1], device_id_type=MESH)
     pl.semaphore_signal(barrier, inc=1, device_id=mate, device_id_type=MESH)
+    for k in range(1, 4):
+        pl.semaphore_signal(barrier, inc=1, device_id=along_y(k)[1], device_id_type=MESH)
+    for k in range(1, 8):
+        pl.semaphore_signal(barrier, inc=1, device_id=along_z(k)[1], device_id_type=MESH)
 
     def give_weights():
         return pltpu.make_async_remote_copy(
-            w2, wpair.at[plane], w_sem.at[0], w_sem.at[1], device_id=mate, device_id_type=MESH
+            w2.at[y], wpair.at[plane, y], w_send.at[0], w_recv.at[0], device_id=mate, device_id_type=MESH
+        )
+
+    def pass_weights(k):
+        return pltpu.make_async_remote_copy(
+            wpair.at[1 - plane, y], wpair.at[1 - plane, y],
+            w_send.at[k], w_recv.at[k], device_id=along_y(k)[1], device_id_type=MESH,
         )
 
     def keep_weights():
-        return pltpu.make_async_copy(w2, wpair.at[plane], w_sem.at[2])
+        return pltpu.make_async_copy(w2, wpair.at[plane], w_send.at[4])
+
+    def scatter_y(kind, k):
+        q, device = along_y(k)
+        return pltpu.make_async_remote_copy(
+            part.at[kind, q], from_y.at[kind, k], y_send.at[kind, k], y_recv.at[kind, k],
+            device_id=device, device_id_type=MESH,
+        )
+
+    def scatter_z(kind, k):
+        q, device = along_z(k)
+        return pltpu.make_async_remote_copy(
+            piece.at[kind, q], from_z.at[kind, k], z_send.at[kind, k], z_recv.at[kind, k],
+            device_id=device, device_id_type=MESH,
+        )
+
+    def gather_z(k):
+        return pltpu.make_async_remote_copy(
+            whole.at[:, zl], whole.at[:, zl], end_send.at[0, k], end_recv.at[0, k],
+            device_id=along_z(k)[1], device_id_type=MESH,
+        )
+
+    def gather_y(k):
+        return pltpu.make_async_remote_copy(
+            whole, every.at[y], end_send.at[1, k], end_recv.at[1, k],
+            device_id=along_y(k)[1], device_id_type=MESH,
+        )
 
     def out_copy(c, k):
         q, device = peer(k)
@@ -103,7 +150,7 @@
         half = dot(swap, w1[i]).astype(BF)
         w1p[i] = dot(half, swap).astype(BF)
     acc_first[...] = jnp.zeros_like(acc_first)
-    pl.semaphore_wait(barrier, 8)
+    pl.semaphore_wait(barrier, 18)
     give_weights().start()
     keep_weights().start()
 
@@ -140,11 +187,16 @@
     lax.fori_loop(0, chunks, begin, 0)
     to_mate(chunks - 1)
 
+    give_weights().wait_recv()
+    for k in range(1, 4):
+        pass_weights(k).start()
+
     rows_q, cols_q = iota((128, 1024), 0), iota((128, 1024), 1)
     sel_ab[...] = (rows_q == column_ab(cols_q, plane)).astype(BF)
     sel_ci[...] = (rows_q == column_ci(cols_q, plane)).astype(BF)
-    give_weights().wait_recv()
     keep_weights().wait()
+    for k in range(1, 4):
+        pass_weights(k).wait_recv()
 
     def spread(b, _):
         start = pl.multiple_of(b * 128, 128)
@@ -220,11 +272,42 @@
     for j in range(4):
         chosen = ((cols_q >> 1) & 7) == plane * 4 + j
         pick = jnp.where(chosen, sel_ci[...].astype(F32), 0.0).astype(BF)
-        second_out[j] = dot(pick, mid[...]).astype(BF)
+        part[1, j] = dot(pick, mid[...]).astype(BF)
+    for k in range(1, 4):
+        scatter_y(1, k).start()
     finish(chunks - 1)
     for i in range(4):
         half = dot(swap, acc_first[i].astype(BF)).astype(BF)
-        first_out[i] = dot(half, swap).astype(BF)
+        part[0, i] = dot(half, swap).astype(BF)
+    for k in range(1, 4):
+        scatter_y(0, k).start()
+    for kind in (1, 0):
+        total = part[kind, y].astype(F32)
+        for k in range(1, 4):
+            scatter_y(kind, k).wait_recv()
+            total += from_y[kind, k].astype(F32)
+        piece[kind] = total.astype(BF).reshape(8, 16, 128)
+        for k in range(1, 8):
+            scatter_z(kind, k).start()
+    for kind in (1, 0):
+        total = piece[kind, zl].astype(F32)
+        for k in range(1, 8):
+            scatter_z(kind, k).wait_recv()
+            total += from_z[kind, k].astype(F32)
+        whole[kind, zl] = total.astype(BF)
+    for k in range(1, 8):
+        gather_z(k).start()
+    for k in range(1, 8):
+        gather_z(k).wait_recv()
+    for k in range(1, 4):
+        gather_y(k).start()
+    first_out[y] = whole[0].reshape(128, 128).astype(F32) * scale
+    second_out[y] = whole[1].reshape(128, 128).astype(F32) * scale
+    for k in range(1, 4):
+        gather_y(k).wait_recv()
+        q = (y + 4 - k) % 4
+        first_out[q] = every[q, 0].reshape(128, 128).astype(F32) * scale
+        second_out[q] = every[q, 1].reshape(128, 128).astype(F32) * scale
 
     def drain(c, _):
         for k in range(1, 8):
@@ -236,6 +319,15 @@
 
     lax.fori_loop(0, chunks, drain, 0)
     give_weights().wait_send()
+    for k in range(1, 4):
+        pass_weights(k).wait_send()
+        scatter_y(0, k).wait_send()
+        scatter_y(1, k).wait_send()
+        gather_y(k).wait_send()
+    for k in range(1, 8):
+        scatter_z(0, k).wait_send()
+        scatter_z(1, k).wait_send()
+        gather_z(k).wait_send()
 
 
 def shards(tokens, cotangent, first_factor, second_factor):
@@ -244,9 +336,9 @@
     n = rows // chunks
     V = pl.BlockSpec(memory_space=pltpu.VMEM)
     dma = pltpu.SemaphoreType.DMA
-    small = jax.ShapeDtypeStruct(first_factor.shape, BF)
+    small = jax.ShapeDtypeStruct(first_factor.shape, F32)
     wide = jax.ShapeDtypeStruct((rows, width), BF)
-    output, input_grad, first, second = pl.pallas_call(
+    return pl.pallas_call(
         lambda *refs: kernel(chunks, *refs),
         out_shape=(wide, wide, small, small),
         in_specs=[V] * 4,
@@ -268,6 +360,12 @@
             pltpu.VMEM((4, 128, 128), F32),
             pltpu.VMEM((1024, 1024), F32),
             pltpu.VMEM((1024, 128), BF),
+            pltpu.VMEM((2, 4, 128, 128), BF),
+            pltpu.VMEM((2, 4, 128, 128), BF),
+            pltpu.VMEM((2, 8, 16, 128), BF),
+            pltpu.VMEM((2, 8, 16, 128), BF),
+            pltpu.VMEM((2, 8, 16, 128), BF),
+            pltpu.VMEM((4, 2, 8, 16, 128), BF),
             dma((chunks, 8)),
             dma((chunks, 8)),
             dma((chunks, 2)),
@@ -275,14 +373,18 @@
             dma((chunks, 8)),
             dma((chunks, 8)),
             dma((chunks, 2)),
-            dma((3,)),
+            dma((5,)),
+            dma((4,)),
+            dma((2, 4)),
+            dma((2, 4)),
+            dma((2, 8)),
+            dma((2, 8)),
+            dma((2, 8)),
+            dma((2, 8)),
         ],
         compiler_params=pltpu.CompilerParams(collective_id=0, has_side_effects=True),
         name="mixing",
     )(tokens, cotangent, first_factor, second_factor)
-    scale = 1.0 / jnp.sqrt(jnp.float32(rows * lax.axis_size("dp")))
-    first_grad, second_grad = lax.psum((first.astype(F32) * scale, second.astype(F32) * scale), "dp")
-    return (output, input_grad, first_grad, second_grad)
 
 
 def solution(mesh):

time: 694 us -> 249 us (0.36)
  the two profiles are of different devices: /device:TPU:2 before, /device:TPU:4 now
where the time goes in v2:
time: 249 us
  Pallas kernels  243 us (98%)
  local copies, waits for them, and re-layouts  5.19 us (2%)
    pallas_call x1, Pallas kernels, shards(): pl.pallas_call(lambda *refs: kernel(chunks, *refs), out_shape=(wide, wide...  243 us
    unnamed x10, local copies, waits for them, and re-layouts  5.19 us

profile of v2, /device:TPU:4, one launch (start us, length us, event | category | flops | bytes accessed | tf_op | source)
XLA Modules:
  0.0 249.2 jit_solution(18074083434239475893)
XLA Ops:
  0.6 243.3 %mixing.1 = (bf16[1024,512]{1,0:T(8,128)(2,1)}, bf16[1024,512]{1,0:T(8,128)(2,1)}, f32[4,128,128]{2,1,0:T(8,128)}, f32[4,128,128]{2,1,0:T(8,128)}) custom-call(bf16[1024,512]{1,0:T(8,128)(2,1)} %refs_0_.1, bf16[1024,512]{1,0:T(8,128)(2,1)} %refs_1_.1, bf16[4,128,128]{2,1,0:T(8,128)(2,1)} %refs_2_.1, bf16[4,128,128]{2,1,0:T(8,128)(2,1)} %refs_3_.1), custom_call_target="tpu_custom_call" | custom-call | tf_op jit(solution)/shard_map/mixing/pallas_call | solution.py:341
  244.0 0.0 copy-start
  244.0 2.4 copy.12
  246.3 0.0 copy-done
  246.3 0.0 copy-start.2
  246.3 1.0 copy.13
  247.3 0.1 copy-done.2
  247.4 0.0 copy-start.1
  247.4 0.7 copy.14
  248.1 0.3 copy-done.1
  248.5 0.7 copy.15
Async XLA Ops:
  244.0 2.4 copy-start
  246.3 1.1 copy-start.2
  247.4 1.0 copy-start.1

commit v3 on v2

--- a/solution.py
+++ b/solution.py
@@ -45,8 +45,8 @@
     tok, cot, w1, w2,
     out, grad_in, first_out, second_out,
     stage, held, back, landed, xt, gt, w1t, w1p, wpair, wf, wb, sel_ab, sel_ci, acc_first, acc_second, mid,
-    part, from_y, piece, from_z, whole, every,
-    send_a, recv_a, send_z, recv_z, send_b, recv_b, own_sem, w_send, w_recv, y_send, y_recv, z_send, z_recv, end_send, end_recv,
+    part, from_y, cross, cross_y, other, piece, from_z, whole, every,
+    send_a, recv_a, send_z, recv_z, send_b, recv_b, own_sem, w_send, w_recv, y_send, y_recv, z_send, z_recv, end_send, end_recv, swap_sem,
 ):
     n = tok.shape[0] // chunks
     d, m = lax.axis_index("dp"), lax.axis_index("mp")
@@ -54,7 +54,7 @@
     me = x * 2 + core
     mate = (d, m + 2 - 4 * plane)
     zl, y = d // 4, d % 4
-    scale = 1.0 / jnp.sqrt(jnp.float32(tok.shape[0] * 32))
+    scale = 1.0 / jnp.sqrt(jnp.float32(tok.shape[0] * lax.axis_size("dp")))
 
     def along_y(k):
         q = (y + k) % 4
@@ -94,8 +94,13 @@
     def scatter_y(kind, k):
         q, device = along_y(k)
         return pltpu.make_async_remote_copy(
-            part.at[kind, q], from_y.at[kind, k], y_send.at[kind, k], y_recv.at[kind, k],
-            device_id=device, device_id_type=MESH,
+            cross.at[:, q] if kind else part.at[q], cross_y.at[k] if kind else from_y.at[k],
+            y_send.at[kind, k], y_recv.at[kind, k], device_id=device, device_id_type=MESH,
+        )
+
+    def swap_planes():
+        return pltpu.make_async_remote_copy(
+            other.at[0], other.at[1], swap_sem.at[0], swap_sem.at[1], device_id=mate, device_id_type=MESH
         )
 
     def scatter_z(kind, k):
@@ -117,15 +122,17 @@
             device_id=along_y(k)[1], device_id_type=MESH,
         )
 
-    def out_copy(c, k):
+    def out_copy(c, kind, k):
         q, device = peer(k)
         return pltpu.make_async_remote_copy(
-            stage.at[c, q], held.at[c, 0, :, pl.ds(4 * me, 4)],
-            send_a.at[c, k], recv_a.at[c, k], device_id=device, device_id_type=MESH,
-        )
-
-    def out_own(c):
-        return pltpu.make_async_copy(stage.at[c, me], held.at[c, 0, :, pl.ds(4 * me, 4)], own_sem.at[c, 0])
+            stage.at[c, kind, q], held.at[c, 0, kind, pl.ds(4 * me, 4)],
+            send_a.at[c, kind, k], recv_a.at[c, kind, k], device_id=device, device_id_type=MESH,
+        )
+
+    def out_own(c, kind):
+        return pltpu.make_async_copy(
+            stage.at[c, kind, me], held.at[c, 0, kind, pl.ds(4 * me, 4)], own_sem.at[c, kind]
+        )
 
     def plane_copy(c, kind):
         return pltpu.make_async_remote_copy(
@@ -133,15 +140,30 @@
             send_z.at[c, kind], recv_z.at[c, kind], device_id=mate, device_id_type=MESH,
         )
 
-    def back_copy(c, k):
+    def back_copy(c, kind, k):
         q, device = peer(k)
         return pltpu.make_async_remote_copy(
-            back.at[c, q], landed.at[c, :, :, me],
-            send_b.at[c, k], recv_b.at[c, k], device_id=device, device_id_type=MESH,
-        )
-
-    def back_own(c):
-        return pltpu.make_async_copy(back.at[c, me], landed.at[c, :, :, me], own_sem.at[c, 1])
+            back.at[c, kind, q], landed.at[c, kind, :, me],
+            send_b.at[c, kind, k], recv_b.at[c, kind, k], device_id=device, device_id_type=MESH,
+        )
+
+    def back_own(c, kind):
+        return pltpu.make_async_copy(back.at[c, kind, me], landed.at[c, kind, :, me], own_sem.at[c, 2 + kind])
+
+    def send_out(c, kind):
+        out_own(c, kind).start()
+        for k in range(1, 8):
+            out_copy(c, kind, k).start()
+
+    def send_back(c, kind):
+        back_own(c, kind).start()
+        for k in range(1, 8):
+            back_copy(c, kind, k).start()
+
+    def await_back(c, kind):
+        for k in range(1, 8):
+            back_copy(c, kind, k).wait_recv()
+        back_own(c, kind).wait()
 
     swap = swap_matrix()
     for i in range(4):
@@ -154,12 +176,11 @@
     give_weights().start()
     keep_weights().start()
 
-    def to_mate(c):
-        for k in range(1, 8):
-            out_copy(c, k).wait_recv()
-        out_own(c).wait()
-        for kind in range(2):
-            plane_copy(c, kind).start()
+    def to_mate(c, kind):
+        for k in range(1, 8):
+            out_copy(c, kind, k).wait_recv()
+        out_own(c, kind).wait()
+        plane_copy(c, kind).start()
 
     def begin(c, _):
         rows = pl.ds(pl.multiple_of(c * n, n), n)
@@ -167,25 +188,25 @@
             cols = pl.ds(128 * i, 128)
             xf = dot(swap, tok[rows, cols], NT)
             gf = dot(swap, cot[rows, cols], NT)
-            xb = xf.astype(BF)
-            xt[c, i] = xb
+            xt[c, i] = xf.astype(BF)
             gt[c, i] = gf.astype(BF)
-            hidden = dot(w1t[i], xb).astype(BF)
             grad_z = (gf * (xf * jax.nn.sigmoid(xf))).astype(BF)
-            stage[c, :, 0, i] = hidden.reshape(8, 16, n)
-            stage[c, :, 1, i] = grad_z.reshape(8, 16, n)
-        out_own(c).start()
-        for k in range(1, 8):
-            out_copy(c, k).start()
+            stage[c, 1, :, i] = grad_z.reshape(8, 16, n)
+        send_out(c, 1)
+        for i in range(4):
+            stage[c, 0, :, i] = dot(w1t[i], xt[c, i]).astype(BF).reshape(8, 16, n)
+        send_out(c, 0)
 
         @pl.when(c >= 1)
         def _():
-            to_mate(c - 1)
+            to_mate(c - 1, 1)
 
         return 0
 
     lax.fori_loop(0, chunks, begin, 0)
-    to_mate(chunks - 1)
+    to_mate(chunks - 1, 1)
+    for c in range(3):
+        to_mate(c, 0)
 
     give_weights().wait_recv()
     for k in range(1, 4):
@@ -220,37 +241,45 @@
     acc_second[...] = jnp.zeros_like(acc_second)
     eye = (iota((n, n), 0) == iota((n, n), 1)).astype(BF)
 
+    def first_term(c):
+        await_back(c, 1)
+        for i in range(4):
+            acc_first[i] += dot(xt[c, i], landed[c, 1, i].reshape(128, n), NT)
+
     def finish(c):
-        for k in range(1, 8):
-            back_copy(c, k).wait_recv()
-        back_own(c).wait()
+        await_back(c, 0)
         rows = pl.ds(pl.multiple_of(c * n, n), n)
         for i in range(4):
             cols = pl.ds(128 * i, 128)
-            xb = xt[c, i]
-            xf = xb.astype(F32)
+            xf = xt[c, i].astype(F32)
             gf = gt[c, i].astype(F32)
             zf = landed[c, 0, i].reshape(128, n).astype(F32)
             gu = landed[c, 1, i].reshape(128, n)
             sig = jax.nn.sigmoid(xf)
-            y = (zf * (xf * sig)).astype(BF)
+            y_part = (zf * (xf * sig)).astype(BF)
             gate = (gf * zf * sig * (1.0 + xf * (1.0 - sig))).astype(BF)
             gx = (dot(w1p[i], gu) + gate.astype(F32)).astype(BF)
-            acc_first[i] += dot(xb, gu, NT)
-            out[rows, cols] = dot(dot(eye, y, NT).astype(BF), swap).astype(BF)
+            out[rows, cols] = dot(dot(eye, y_part, NT).astype(BF), swap).astype(BF)
             grad_in[rows, cols] = dot(dot(eye, gx, NT).astype(BF), swap).astype(BF)
 
-    def middle(c, _):
-        for kind in range(2):
-            plane_copy(c, kind).wait_recv()
+    def backward(c, _):
+        plane_copy(c, 1).wait_recv()
+        grad_mixed = held[c, :, 1].reshape(1024, n)
+        back[c, 1] = dot(wb[...], grad_mixed).astype(BF).reshape(8, 4, 16, n)
+        send_back(c, 1)
+        acc_second[...] += dot(held[c, 0, 0].reshape(512, n), grad_mixed, NT)
+
+        @pl.when(c >= 1)
+        def _():
+            first_term(c - 1)
+
+        return 0
+
+    def forward(c, _):
+        plane_copy(c, 0).wait_recv()
         hidden = held[c, :, 0].reshape(1024, n)
-        grad_mixed = held[c, :, 1].reshape(1024, n)
-        back[c, :, 0] = dot(wf[...], hidden).astype(BF).reshape(8, 4, 16, n)
-        back[c, :, 1] = dot(wb[...], grad_mixed).astype(BF).reshape(8, 4, 16, n)
-        back_own(c).start()
-        for k in range(1, 8):
-            back_copy(c, k).start()
-        acc_second[...] += dot(hidden, grad_mixed, NT)
+        back[c, 0] = dot(wf[...], hidden).astype(BF).reshape(8, 4, 16, n)
+        send_back(c, 0)
 
         @pl.when(c >= 1)
         def _():
@@ -258,38 +287,63 @@
 
         return 0
 
-    lax.fori_loop(0, chunks, middle, 0)
+    def own_hidden(c, _):
+        for k in range(1, 8):
+            out_copy(c, 0, k).wait_recv()
+        out_own(c, 0).wait()
+        return 0
+
+    lax.fori_loop(3, chunks, own_hidden, 0)
+    lax.fori_loop(0, chunks, backward, 0)
 
     def gather(b, _):
         start = pl.multiple_of(b * 128, 128)
         code = iota((128, 1024), 0)
         same = ((code >> 1) & 7) == ((cols_q >> 1) & 7)
-        part = jnp.where(same, acc_second[pl.ds(start, 128)], 0.0).astype(BF)
-        mid[pl.ds(start, 128)] = dot(part, sel_ab[...], NT).astype(BF)
-        return 0
-
-    lax.fori_loop(0, 8, gather, 0)
-    for j in range(4):
-        chosen = ((cols_q >> 1) & 7) == plane * 4 + j
-        pick = jnp.where(chosen, sel_ci[...].astype(F32), 0.0).astype(BF)
-        part[1, j] = dot(pick, mid[...]).astype(BF)
+        row_part = jnp.where(same, acc_second[pl.ds(start, 128)], 0.0).astype(BF)
+        mid[pl.ds(start, 128)] = dot(row_part, sel_ab[...], NT).astype(BF)
+        return 0
+
+    lax.fori_loop(0, 4, gather, 0)
+    rows_s, cols_s = iota((64, 512), 0), iota((64, 512), 1)
+    aligned = ((cols_s >> 4) == (rows_s & 31)) & ((cols_s & 1) == (rows_s >> 5))
+    for j in range(8):
+        pick = (aligned & (((cols_s >> 1) & 7) == j)).astype(BF)
+        cross[j // 4, j % 4] = dot(pick, mid[...]).astype(BF)
     for k in range(1, 4):
         scatter_y(1, k).start()
-    finish(chunks - 1)
+    first_term(chunks - 1)
     for i in range(4):
         half = dot(swap, acc_first[i].astype(BF)).astype(BF)
-        part[0, i] = dot(half, swap).astype(BF)
+        part[i] = dot(half, swap).astype(BF)
     for k in range(1, 4):
         scatter_y(0, k).start()
-    for kind in (1, 0):
-        total = part[kind, y].astype(F32)
-        for k in range(1, 4):
-            scatter_y(kind, k).wait_recv()
-            total += from_y[kind, k].astype(F32)
-        piece[kind] = total.astype(BF).reshape(8, 16, 128)
-        for k in range(1, 8):
-            scatter_z(kind, k).start()
-    for kind in (1, 0):
+    kept = cross[plane, y].astype(F32)
+    given = cross[1 - plane, y].astype(F32)
+    for k in range(1, 4):
+        scatter_y(1, k).wait_recv()
+        kept += cross_y[k, plane].astype(F32)
+        given += cross_y[k, 1 - plane].astype(F32)
+    other[0] = given.astype(BF)
+    swap_planes().start()
+    piece[1, pl.ds(4 * plane, 4)] = kept.astype(BF).reshape(4, 16, 128)
+    total = part[y].astype(F32)
+    for k in range(1, 4):
+        scatter_y(0, k).wait_recv()
+        total += from_y[k].astype(F32)
+    piece[0] = total.astype(BF).reshape(8, 16, 128)
+    for k in range(1, 8):
+        scatter_z(0, k).start()
+    for c in range(3, 5):
+        plane_copy(c, 0).start()
+    lax.fori_loop(0, 1, forward, 0)
+    swap_planes().wait_recv()
+    piece[1, pl.ds(4 - 4 * plane, 4)] = other[1].reshape(4, 16, 128)
+    for k in range(1, 8):
+        scatter_z(1, k).start()
+    plane_copy(5, 0).start()
+    lax.fori_loop(1, 2, forward, 0)
+    for kind in range(2):
         total = piece[kind, zl].astype(F32)
         for k in range(1, 8):
             scatter_z(kind, k).wait_recv()
@@ -297,28 +351,43 @@
         whole[kind, zl] = total.astype(BF)
     for k in range(1, 8):
         gather_z(k).start()
+    for c in range(6, chunks):
+        plane_copy(c, 0).start()
+    lax.fori_loop(2, 5, forward, 0)
     for k in range(1, 8):
         gather_z(k).wait_recv()
     for k in range(1, 4):
         gather_y(k).start()
-    first_out[y] = whole[0].reshape(128, 128).astype(F32) * scale
-    second_out[y] = whole[1].reshape(128, 128).astype(F32) * scale
+    lax.fori_loop(5, 6, forward, 0)
+
+    row, col = iota((128, 128), 0), iota((128, 128), 1)
+    ordered = ((row >> 3) & 1) * 64 + (row >> 6) * 32 + ((row >> 4) & 3) * 8 + (row & 7)
+    restore = (col == ordered).astype(BF)
+
+    def emit(q, summed):
+        first_out[q] = summed[0].reshape(128, 128).astype(F32) * scale
+        second_out[q] = dot(restore, summed[1].reshape(128, 128)) * scale
+
+    emit(y, whole)
     for k in range(1, 4):
         gather_y(k).wait_recv()
         q = (y + 4 - k) % 4
-        first_out[q] = every[q, 0].reshape(128, 128).astype(F32) * scale
-        second_out[q] = every[q, 1].reshape(128, 128).astype(F32) * scale
+        emit(q, every.at[q])
+    lax.fori_loop(6, chunks, forward, 0)
+    finish(chunks - 1)
 
     def drain(c, _):
         for k in range(1, 8):
-            out_copy(c, k).wait_send()
-            back_copy(c, k).wait_send()
+            for kind in range(2):
+                out_copy(c, kind, k).wait_send()
+                back_copy(c, kind, k).wait_send()
         for kind in range(2):
             plane_copy(c, kind).wait_send()
         return 0
 
     lax.fori_loop(0, chunks, drain, 0)
     give_weights().wait_send()
+    swap_planes().wait_send()
     for k in range(1, 4):
         pass_weights(k).wait_send()
         scatter_y(0, k).wait_send()
@@ -344,9 +413,9 @@
         in_specs=[V] * 4,
         out_specs=(V,) * 4,
         scratch_shapes=[
-            pltpu.VMEM((chunks, 8, 2, 4, 16, n), BF),
+            pltpu.VMEM((chunks, 2, 8, 4, 16, n), BF),
             pltpu.VMEM((chunks, 2, 2, 32, 16, n), BF),
-            pltpu.VMEM((chunks, 8, 2, 4, 16, n), BF),
+            pltpu.VMEM((chunks, 2, 8, 4, 16, n), BF),
             pltpu.VMEM((chunks, 2, 4, 8, 16, n), BF),
             pltpu.VMEM((chunks, 4, 128, n), BF),
             pltpu.VMEM((chunks, 4, 128, n), BF),
@@ -358,21 +427,24 @@
             pltpu.VMEM((128, 1024), BF),
             pltpu.VMEM((128, 1024), BF),
             pltpu.VMEM((4, 128, 128), F32),
-            pltpu.VMEM((1024, 1024), F32),
-            pltpu.VMEM((1024, 128), BF),
-            pltpu.VMEM((2, 4, 128, 128), BF),
-            pltpu.VMEM((2, 4, 128, 128), BF),
+            pltpu.VMEM((512, 1024), F32),
+            pltpu.VMEM((512, 128), BF),
+            pltpu.VMEM((4, 128, 128), BF),
+            pltpu.VMEM((4, 128, 128), BF),
+            pltpu.VMEM((2, 4, 64, 128), BF),
+            pltpu.VMEM((4, 2, 64, 128), BF),
+            pltpu.VMEM((2, 64, 128), BF),
             pltpu.VMEM((2, 8, 16, 128), BF),
             pltpu.VMEM((2, 8, 16, 128), BF),
             pltpu.VMEM((2, 8, 16, 128), BF),
             pltpu.VMEM((4, 2, 8, 16, 128), BF),
-            dma((chunks, 8)),
-            dma((chunks, 8)),
+            dma((chunks, 2, 8)),
+            dma((chunks, 2, 8)),
             dma((chunks, 2)),
             dma((chunks, 2)),
-            dma((chunks, 8)),
-            dma((chunks, 8)),
-            dma((chunks, 2)),
+            dma((chunks, 2, 8)),
+            dma((chunks, 2, 8)),
+            dma((chunks, 4)),
             dma((5,)),
             dma((4,)),
             dma((2, 4)),
@@ -381,6 +453,7 @@
             dma((2, 8)),
             dma((2, 8)),
             dma((2, 8)),
+            dma((2,)),
         ],
         compiler_params=pltpu.CompilerParams(collective_id=0, has_side_effects=True),
         name="mixing",

time: 249 us -> 242 us (0.972)
  the two profiles are of different devices: /device:TPU:4 before, /device:TPU:69 now
where the time goes in v3:
time: 242 us
  Pallas kernels  236 us (98%)
  local copies, waits for them, and re-layouts  5.19 us (2%)
    pallas_call x1, Pallas kernels, shards(): pl.pallas_call(lambda *refs: kernel(chunks, *refs), out_shape=(wide, wide...  236 us
    unnamed x10, local copies, waits for them, and re-layouts  5.19 us

profile of v3, /device:TPU:69, one launch (start us, length us, event | category | flops | bytes accessed | tf_op | source)
XLA Modules:
  0.0 241.7 jit_solution(512452979556133238)
XLA Ops:
  0.6 235.8 %mixing.1 = (bf16[1024,512]{1,0:T(8,128)(2,1)}, bf16[1024,512]{1,0:T(8,128)(2,1)}, f32[4,128,128]{2,1,0:T(8,128)}, f32[4,128,128]{2,1,0:T(8,128)}) custom-call(bf16[1024,512]{1,0:T(8,128)(2,1)} %refs_0_.1, bf16[1024,512]{1,0:T(8,128)(2,1)} %refs_1_.1, bf16[4,128,128]{2,1,0:T(8,128)(2,1)} %refs_2_.1, bf16[4,128,128]{2,1,0:T(8,128)(2,1)} %refs_3_.1), custom_call_target="tpu_custom_call" | custom-call | tf_op jit(solution)/shard_map/mixing/pallas_call | solution.py:410
  236.5 0.0 copy-start
  236.5 2.4 copy.12
  238.8 0.0 copy-done
  238.8 0.0 copy-start.2
  238.8 1.0 copy.13
  239.8 0.1 copy-done.2
  239.9 0.0 copy-start.1
  239.9 0.7 copy.14
  240.6 0.3 copy-done.1
  241.0 0.7 copy.15
Async XLA Ops:
  236.5 2.4 copy-start
  238.8 1.1 copy-start.2
  239.9 1.0 copy-start.1

commit v4 on v3

--- a/solution.py
+++ b/solution.py
@@ -44,7 +44,7 @@
     chunks,
     tok, cot, w1, w2,
     out, grad_in, first_out, second_out,
-    stage, held, back, landed, xt, gt, w1t, w1p, wpair, wf, wb, sel_ab, sel_ci, acc_first, acc_second, mid,
+    stage, held, back, landed, xt, gt, silu, slope, base, w1t, w1p, wpair, wf, wb, sel_ab, sel_ci, acc_first, acc_second, mid,
     part, from_y, cross, cross_y, other, piece, from_z, whole, every,
     send_a, recv_a, send_z, recv_z, send_b, recv_b, own_sem, w_send, w_recv, y_send, y_recv, z_send, z_recv, end_send, end_recv, swap_sem,
 ):
@@ -172,8 +172,6 @@
         half = dot(swap, w1[i]).astype(BF)
         w1p[i] = dot(half, swap).astype(BF)
     acc_first[...] = jnp.zeros_like(acc_first)
-    pl.semaphore_wait(barrier, 18)
-    give_weights().start()
     keep_weights().start()
 
     def to_mate(c, kind):
@@ -182,7 +180,7 @@
         out_own(c, kind).wait()
         plane_copy(c, kind).start()
 
-    def begin(c, _):
+    def prepare(c):
         rows = pl.ds(pl.multiple_of(c * n, n), n)
         for i in range(4):
             cols = pl.ds(128 * i, 128)
@@ -192,20 +190,28 @@
             gt[c, i] = gf.astype(BF)
             grad_z = (gf * (xf * jax.nn.sigmoid(xf))).astype(BF)
             stage[c, 1, :, i] = grad_z.reshape(8, 16, n)
-        send_out(c, 1)
+
+    def prepare_hidden(c):
         for i in range(4):
             stage[c, 0, :, i] = dot(w1t[i], xt[c, i]).astype(BF).reshape(8, 16, n)
+
+    def begin(c, _):
+        prepare(c)
+        send_out(c, 1)
+        prepare_hidden(c)
         send_out(c, 0)
-
-        @pl.when(c >= 1)
-        def _():
-            to_mate(c - 1, 1)
-
-        return 0
-
-    lax.fori_loop(0, chunks, begin, 0)
+        to_mate(c - 1, 1)
+        return 0
+
+    prepare(0)
+    prepare_hidden(0)
+    pl.semaphore_wait(barrier, 18)
+    send_out(0, 1)
+    give_weights().start()
+    send_out(0, 0)
+    lax.fori_loop(1, chunks, begin, 0)
     to_mate(chunks - 1, 1)
-    for c in range(3):
+    for c in range(2):
         to_mate(c, 0)
 
     give_weights().wait_recv()
@@ -244,21 +250,23 @@
     def first_term(c):
         await_back(c, 1)
         for i in range(4):
-            acc_first[i] += dot(xt[c, i], landed[c, 1, i].reshape(128, n), NT)
+            gu = landed[c, 1, i].reshape(128, n)
+            acc_first[i] += dot(xt[c, i], gu, NT)
+            base[c, i] = dot(w1p[i], gu)
+            xf = xt[c, i].astype(F32)
+            sig = jax.nn.sigmoid(xf)
+            silu[c, i] = xf * sig
+            slope[c, i] = gt[c, i].astype(F32) * sig * (1.0 + xf * (1.0 - sig))
 
     def finish(c):
         await_back(c, 0)
         rows = pl.ds(pl.multiple_of(c * n, n), n)
         for i in range(4):
             cols = pl.ds(128 * i, 128)
-            xf = xt[c, i].astype(F32)
-            gf = gt[c, i].astype(F32)
             zf = landed[c, 0, i].reshape(128, n).astype(F32)
-            gu = landed[c, 1, i].reshape(128, n)
-            sig = jax.nn.sigmoid(xf)
-            y_part = (zf * (xf * sig)).astype(BF)
-            gate = (gf * zf * sig * (1.0 + xf * (1.0 - sig))).astype(BF)
-            gx = (dot(w1p[i], gu) + gate.astype(F32)).astype(BF)
+            y_part = (zf * silu[c, i]).astype(BF)
+            gate = (zf * slope[c, i]).astype(BF)
+            gx = (base[c, i] + gate.astype(F32)).astype(BF)
             out[rows, cols] = dot(dot(eye, y_part, NT).astype(BF), swap).astype(BF)
             grad_in[rows, cols] = dot(dot(eye, gx, NT).astype(BF), swap).astype(BF)
 
@@ -293,7 +301,7 @@
         out_own(c, 0).wait()
         return 0
 
-    lax.fori_loop(3, chunks, own_hidden, 0)
+    lax.fori_loop(2, chunks, own_hidden, 0)
     lax.fori_loop(0, chunks, backward, 0)
 
     def gather(b, _):
@@ -334,14 +342,14 @@
     piece[0] = total.astype(BF).reshape(8, 16, 128)
     for k in range(1, 8):
         scatter_z(0, k).start()
-    for c in range(3, 5):
+    for c in range(2, 4):
         plane_copy(c, 0).start()
     lax.fori_loop(0, 1, forward, 0)
     swap_planes().wait_recv()
     piece[1, pl.ds(4 - 4 * plane, 4)] = other[1].reshape(4, 16, 128)
     for k in range(1, 8):
         scatter_z(1, k).start()
-    plane_copy(5, 0).start()
+    plane_copy(4, 0).start()
     lax.fori_loop(1, 2, forward, 0)
     for kind in range(2):
         total = piece[kind, zl].astype(F32)
@@ -351,14 +359,14 @@
         whole[kind, zl] = total.astype(BF)
     for k in range(1, 8):
         gather_z(k).start()
-    for c in range(6, chunks):
+    for c in range(5, chunks):
         plane_copy(c, 0).start()
-    lax.fori_loop(2, 5, forward, 0)
+    lax.fori_loop(2, 4, forward, 0)
     for k in range(1, 8):
         gather_z(k).wait_recv()
     for k in range(1, 4):
         gather_y(k).start()
-    lax.fori_loop(5, 6, forward, 0)
+    lax.fori_loop(4, 5, forward, 0)
 
     row, col = iota((128, 128), 0), iota((128, 128), 1)
     ordered = ((row >> 3) & 1) * 64 + (row >> 6) * 32 + ((row >> 4) & 3) * 8 + (row & 7)
@@ -373,7 +381,7 @@
         gather_y(k).wait_recv()
         q = (y + 4 - k) % 4
         emit(q, every.at[q])
-    lax.fori_loop(6, chunks, forward, 0)
+    lax.fori_loop(5, chunks, forward, 0)
     finish(chunks - 1)
 
     def drain(c, _):
@@ -419,6 +427,9 @@
             pltpu.VMEM((chunks, 2, 4, 8, 16, n), BF),
             pltpu.VMEM((chunks, 4, 128, n), BF),
             pltpu.VMEM((chunks, 4, 128, n), BF),
+            pltpu.VMEM((chunks, 4, 128, n), F32),
+            pltpu.VMEM((chunks, 4, 128, n), F32),
+            pltpu.VMEM((chunks, 4, 128, n), F32),
             pltpu.VMEM((4, 128, 128), BF),
             pltpu.VMEM((4, 128, 128), BF),
             pltpu.VMEM((2, 4, 128, 128), BF),

time: 242 us -> 265 us (1.095)
  the two profiles are of different devices: /device:TPU:69 before, /device:TPU:33 now
where the time goes in v4:
time: 265 us
  Pallas kernels  259 us (98%)
  local copies, waits for them, and re-layouts  5.19 us (2%)
    pallas_call x1, Pallas kernels, shards(): pl.pallas_call(lambda *refs: kernel(chunks, *refs), out_shape=(wide, wide...  259 us

profile of v4, /device:TPU:33, one launch (start us, length us, event | category | flops | bytes accessed | tf_op | source)
XLA Modules:
  0.0 264.7 jit_solution(12616471658734496755)
XLA Ops:
  0.6 258.8 %mixing.1 = (bf16[1024,512]{1,0:T(8,128)(2,1)}, bf16[1024,512]{1,0:T(8,128)(2,1)}, f32[4,128,128]{2,1,0:T(8,128)}, f32[4,128,128]{2,1,0:T(8,128)}) custom-call(bf16[1024,512]{1,0:T(8,128)(2,1)} %refs_0_.1, bf16[1024,512]{1,0:T(8,128)(2,1)} %refs_1_.1, bf16[4,128,128]{2,1,0:T(8,128)(2,1)} %refs_2_.1, bf16[4,128,128]{2,1,0:T(8,128)(2,1)} %refs_3_.1), custom_call_target="tpu_custom_call" | custom-call | tf_op jit(solution)/shard_map/mixing/pallas_call | solution.py:418
  259.5 0.0 copy-start
  259.5 2.4 copy.12
  261.8 0.0 copy-done
  261.8 0.0 copy-start.2
  261.8 1.0 copy.13
  262.8 0.1 copy-done.2
  262.9 0.0 copy-start.1
  262.9 0.7 copy.14
  263.6 0.3 copy-done.1
  264.0 0.7 copy.15
Async XLA Ops:
  259.5 2.4 copy-start
  261.8 1.1 copy-start.2
  262.9 1.0 copy-start.1
